TPU v7x, 32 devices: a whole 2x2x4 slice. The times are simulated.
32 devices in a mesh: groups: 1, seq: 32 (over z, y, x, core).
Axes of the slice: x: 2, y: 2, z: 4, core: 2. Of those that a mesh axis runs over, the one named last changes fastest.
Arguments:
- tokens: bfloat16 [4096, 1536], P(('groups', 'seq')), may hold values from -6 to 6
- state_rates: float32 [2, 64], replicated, may hold values from -40 to 40, as said below
- coupling: float32 [2, 64], replicated, may hold values from -6 to 6
- in_proj: float32 [2, 64, 1536], replicated, may hold values from -120 to 120
- out_proj: float32 [2, 64, 1536], replicated, may hold values from -0.01171875 to 0.01171875
- skip_gain: float32 [1536], replicated, may hold values from -4 to 4
- mix_weight: bfloat16 [1536, 3072], P('seq'), may hold values from -0.15625 to 0.15625
Outputs:
- glu_output: bfloat16 [4096, 1536], P(('groups', 'seq'))
Inputs may be any that keep to these rules, and one draw needn't show every extreme that they name: state_rates[0] is negative, between -12 and -1 / 4096; state_rates[1] lies within -40 to 40.
All inputs are finite; a program needn't handle non-finite values.
Results may differ from a plain program's by a relative error of at most 0.0051.
Values may be sent and summed in bfloat16 or wider, within the bound.
No kernel may reach another device: no remote copies, remote signals or barrier semaphores. Data moves between devices by JAX's collectives and lax.ppermute only.
A program may use at most 64 MiB of HBM per device.

v0:
```python
import math
import jax
import jax.numpy as jnp
from jax import lax
from jax.sharding import PartitionSpec as P

PRECISE = lax.Precision.HIGHEST


def phase_of(numerator, period):
    wrapped = numerator % period
    wrapped = jnp.where(wrapped > period // 2, wrapped - period, wrapped)
    return wrapped.astype(jnp.float32) * (-2.0 * math.pi / period)


def complex_mul(first, second):
    return (
        first[0] * second[0] - first[1] * second[1],
        first[0] * second[1] + first[1] * second[0],
    )


def complex_div(first, second):
    norm_sq = second[0] * second[0] + second[1] * second[1]
    return (
        (first[0] * second[0] + first[1] * second[1]) / norm_sq,
        (first[1] * second[0] - first[0] * second[1]) / norm_sq,
    )


def real_form(pair_real, pair_imag):
    upper = jnp.concatenate([pair_real, pair_imag], axis=1)
    lower = jnp.concatenate([-pair_imag, pair_real], axis=1)
    return jnp.concatenate([upper, lower], axis=0)


def cauchy_right(coupling, in_proj, out_proj):
    in_pair = (in_proj[0], in_proj[1])
    out_pair = (out_proj[0], out_proj[1])
    low_pair = (coupling[0][:, None], coupling[1][:, None])
    low_conj = (low_pair[0], -low_pair[1])
    pair_cb = complex_mul(out_pair, in_pair)
    pair_cp = complex_mul(out_pair, low_pair)
    pair_pb = complex_mul(low_conj, in_pair)
    pair_pp = low_pair[0] * low_pair[0] + low_pair[1] * low_pair[1]
    return [
        real_form(pair_cb[0], pair_cb[1]),
        real_form(pair_cp[0], pair_cp[1]),
        real_form(pair_pb[0], pair_pb[1]),
        real_form(pair_pp, jnp.zeros_like(pair_pp)),
    ]


def response(frequency, full_len, state_rates, right_list):
    half_turn = 0.5 * phase_of(frequency, full_len)
    cos_half = jnp.cos(half_turn)[:, None]
    sin_half = jnp.sin(half_turn)[:, None]
    decay_rate = -state_rates[0][None, :]
    spin_rate = state_rates[1][None, :]
    real_part = cos_half * decay_rate
    imag_part = -(2.0 * sin_half + cos_half * spin_rate)
    inv_norm = 1.0 / (real_part * real_part + imag_part * imag_part)
    cauchy_left = jnp.concatenate([real_part * inv_norm, -imag_part * inv_norm], axis=1)
    term_list = []
    for matrix in right_list:
        summed = jnp.dot(cauchy_left, matrix, precision=PRECISE)
        half_cols = matrix.shape[1] // 2
        term_list.append((summed[:, :half_cols], summed[:, half_cols:]))
    term_cb, term_cp, term_pb, term_pp = term_list
    numerator = complex_mul(term_cp, term_pb)
    denominator = (1.0 + cos_half * term_pp[0], cos_half * term_pp[1])
    fraction = complex_div(numerator, denominator)
    bracket = (term_cb[0] - cos_half * fraction[0], term_cb[1] - cos_half * fraction[1])
    return complex_mul((cos_half, -sin_half), bracket)


def dft_table_of(length, direction):
    position = jnp.arange(length, dtype=jnp.int32)
    phases = phase_of(direction * position[:, None] * position[None, :], length)
    cos_table = jnp.cos(phases)
    sin_table = jnp.sin(phases)
    return jnp.stack(
        [jnp.stack([cos_table, -sin_table], 1), jnp.stack([sin_table, cos_table], 1)], 0
    )


def transform(signal, length, direction):
    return jnp.einsum("ascb,ckbh->aksh", dft_table_of(length, direction), signal, precision=PRECISE)


def block_tables(seq_count):
    block_index = jnp.arange(seq_count, dtype=jnp.int32)
    pair_index = jnp.arange(2 * seq_count, dtype=jnp.int32)
    forward_phase = phase_of(pair_index[:, None] * block_index[None, :], 2 * seq_count)
    forward_table = jnp.concatenate([jnp.cos(forward_phase), jnp.sin(forward_phase)], 0)
    inverse_phase = phase_of(-(block_index[:, None] * pair_index[None, :]), 2 * seq_count)
    inverse_table = jnp.concatenate([jnp.cos(inverse_phase), -jnp.sin(inverse_phase)], 1)
    return (forward_table, inverse_table)


def twiddled(signal, first_index, second_index, full_len, direction):
    phases = phase_of(direction * first_index[:, None] * second_index[None, :], full_len)[
        :, :, None
    ]
    turned = complex_mul((signal[0], signal[1]), (jnp.cos(phases), jnp.sin(phases)))
    return jnp.stack(turned)


def shards(tokens, state_rates, coupling, in_proj, out_proj, skip_gain, mix_weight):
    seq_count = lax.axis_size("seq")
    seq_place = lax.axis_index("seq")
    tok_rows, channels = tokens.shape
    full_len = 2 * tok_rows * seq_count
    forward_table, inverse_table = block_tables(seq_count)
    pair_index = jnp.arange(2 * seq_count, dtype=jnp.int32)
    all_times = jnp.arange(tok_rows, dtype=jnp.int32)
    per_device = tok_rows // seq_count
    columns = lax.all_to_all(tokens[None], "seq", split_axis=1, concat_axis=0, tiled=True)
    spread = jnp.dot(
        forward_table,
        columns.astype(jnp.float32).reshape(seq_count, per_device * channels),
        precision=PRECISE,
    )
    spread = spread.reshape(2, 2 * seq_count, per_device, channels)
    local_time = seq_place * per_device + jnp.arange(per_device, dtype=jnp.int32)
    spread = twiddled(spread, pair_index, local_time, full_len, 1)
    gathered = lax.all_to_all(spread, "seq", split_axis=1, concat_axis=2, tiled=True)
    spectrum = transform(gathered, tok_rows, 1)
    pair_here = 2 * seq_place + jnp.arange(2, dtype=jnp.int32)
    frequency = (pair_here[:, None] + 2 * seq_count * all_times[None, :]).reshape(-1)
    right_list = cauchy_right(coupling, in_proj, out_proj)
    kernel_real, kernel_imag = response(frequency, full_len, state_rates, right_list)
    kernel_pair = (
        kernel_real.reshape(2, tok_rows, channels),
        kernel_imag.reshape(2, tok_rows, channels),
    )
    product = jnp.stack(complex_mul(kernel_pair, (spectrum[0], spectrum[1])))
    inverse = transform(product, tok_rows, -1)
    inverse = twiddled(inverse, pair_here, all_times, full_len, -1)
    returned = lax.all_to_all(inverse, "seq", split_axis=2, concat_axis=1, tiled=True)
    conv_out = jnp.dot(
        inverse_table, returned.reshape(4 * seq_count, per_device * channels), precision=PRECISE
    )
    conv_out = conv_out.reshape(seq_count, per_device, channels) * (1.0 / full_len)
    pre_act = conv_out + skip_gain * columns.astype(jnp.float32)
    activation = jax.nn.gelu(pre_act, approximate=False).astype(jnp.bfloat16)
    act_rows = lax.all_to_all(activation, "seq", split_axis=0, concat_axis=1, tiled=True)[0]
    projected = jnp.dot(
        act_rows,
        lax.all_gather(mix_weight, "seq", axis=0, tiled=True),
        preferred_element_type=jnp.float32,
    )
    return (projected[:, :channels] * jax.nn.sigmoid(projected[:, channels:])).astype(jnp.bfloat16)


def solution(mesh):
    placed = (P(("groups", "seq"), None), P(), P(), P(), P(), P(), P("seq", None))
    return jax.shard_map(
        shards, mesh=mesh, in_specs=placed, out_specs=P(("groups", "seq"), None), check_vma=False
    )
```

profile of v0, /device:TPU:0, one launch (start us, length us, event | category | flops | bytes accessed | tf_op | source)
XLA Modules:
  0.0 290.9 jit_solution(13883926220681180937)
XLA Ops:
  8.7 3.0 %reduce.4 = bf16[128,1536]{1,0:T(8,128)(2,1)S(1)} reduce(bf16[128,1,1536]{2,1,0:T(2,128)(2,1)S(1)} %bitcast.155, bf16[]{:T(256)} %broadcast.842), dimensions={1}, to_apply=%bitcast.146.reduce_sub_computation | reduce | bytes 786434
  12.7 7.3 %all-to-all-start = ((bf16[32,2,3072]{2,1,0:T(2,128)(2,1)}), bf16[32,2,3072]{2,1,0:T(2,128)(2,1)S(1)}, u32[]{:S(2)}, u32[]{:S(2)}) async-start(bf16[32,2,3072]{2,1,0:T(2,128)(2,1)} %reshape.574), calls=%async_computation | async-start | bytes 786432 | tf_op jit(solution)/shard_map/all_to_all | solution.py:118
  21.2 12.1 %all-to-all-done = bf16[32,2,3072]{2,1,0:T(2,128)(2,1)S(1)} async-done(((bf16[32,2,3072]{2,1,0:T(2,128)(2,1)}), bf16[32,2,3072]{2,1,0:T(2,128)(2,1)S(1)}, u32[]{:S(2)}, u32[]{:S(2)}) %all-to-all-start) | async-done | bytes 393248 | tf_op jit(solution)/shard_map/all_to_all | solution.py:118
  40.1 2.4 squeeze.30
  43.3 2.5 pad_maximum_fusion
  45.8 3.1 %all-to-all-start.1 = ((f32[2,64,4,1536]{3,2,0,1:T(4,128)}), f32[2,64,4,1536]{3,2,0,1:T(4,128)S(1)}, u32[]{:S(2)}, u32[]{:S(2)}) async-start(f32[2,64,4,1536]{3,2,0,1:T(4,128)} %pad_maximum_fusion), calls=%async_computation.1 | async-start | bytes 6291456 | tf_op jit(solution)/shard_map/all_to_all | solution.py:127
  51.1 2.7 fusion.12
  53.8 2.7 fusion.20
  56.5 2.7 fusion.4
  63.5 3.0 %copy.80 = f32[1,2,128,1536]{2,3,0,1:T(8,128)} copy(f32[1,2,128,1536]{3,2,1,0:T(8,128)} %bitcast.152) | data formatting | bytes 3145728 | tf_op jit(solution)/shard_map/reshape | solution.py:135
  66.6 3.0 %copy.79 = f32[1,2,128,1536]{2,3,0,1:T(8,128)} copy(f32[1,2,128,1536]{3,2,1,0:T(8,128)} %bitcast.153) | data formatting | bytes 3145728 | tf_op jit(solution)/shard_map/reshape | solution.py:134
  71.3 86.4 %all-to-all-done.1 = f32[2,64,4,1536]{3,2,0,1:T(4,128)S(1)} async-done(((f32[2,64,4,1536]{3,2,0,1:T(4,128)}), f32[2,64,4,1536]{3,2,0,1:T(4,128)S(1)}, u32[]{:S(2)}, u32[]{:S(2)}) %all-to-all-start.1) | async-done | bytes 3145760 | tf_op jit(solution)/shard_map/all_to_all | solution.py:127
  157.7 2.6 copy.77
  160.4 5.1 %convolution_bitcast_fusion.1 = f32[2,2,128,1536]{2,3,0,1:T(8,128)S(1)} fusion(f32[2,2,128,1536,1]{3,1,2,0,4:T(2,128)S(1)} %bitcast.149, f32[1,128,2,128]{3,1,2,0:T(8,128)S(1)} %get-tuple-element.41, f32[1,128,2,128]{3,1,2,0:T(8,128)S(1)} %get-tuple-element.40), kind=kOutput, calls=%fused_computation.1 | convolution fusion | flops 2415984640 | bytes 6553600 | tf_op jit(solution)/shard_map/ascb,ckbh->aksh/dot_general | solution.py:88
  166.4 2.8 convolution_bitcast_fusion
  169.8 3.6 %copy.83 = f32[2,2,128,1536]{3,0,1,2:T(2,128)} copy(f32[2,2,128,1536]{2,3,0,1:T(8,128)S(1)} %pad_maximum_fusion.1) | data formatting | bytes 6291456 | tf_op jit(solution)/shard_map/stack | solution.py:106
  173.3 3.8 %all-to-all-start.2 = ((f32[2,2,128,1536]{3,0,1,2:T(2,128)}), f32[2,2,128,1536]{3,0,1,2:T(2,128)S(1)}, u32[]{:S(2)}, u32[]{:S(2)}) async-start(f32[2,2,128,1536]{3,0,1,2:T(2,128)} %copy.83), calls=%async_computation.2 | async-start | bytes 6291456 | tf_op jit(solution)/shard_map/all_to_all | solution.py:140
  177.3 4.3 %convert_reduce_fusion = f32[128,1536]{1,0:T(8,128)} fusion(bf16[128,1,1536]{2,1,0:T(2,128)(2,1)} %copy-done), kind=kLoop, calls=%fused_computation.60 | loop fusion | flops 196608 | bytes 1179648 | tf_op jit(solution)/shard_map/convert_element_type | solution.py:121
  181.5 2.3 reshape.564
  183.8 64.7 %all-to-all-done.2 = f32[2,2,128,1536]{3,0,1,2:T(2,128)S(1)} async-done(((f32[2,2,128,1536]{3,0,1,2:T(2,128)}), f32[2,2,128,1536]{3,0,1,2:T(2,128)S(1)}, u32[]{:S(2)}, u32[]{:S(2)}) %all-to-all-start.2) | async-done | bytes 3145760 | tf_op jit(solution)/shard_map/all_to_all | solution.py:140
  250.7 2.4 copy.86
  253.1 6.9 %fusion.32 = bf16[32,4,1536]{2,0,1:T(8,128)(2,1)S(1)} fusion(f32[32,4,1536]{2,1,0:T(4,128)} %reshape.564, f32[4,1536,128]{2,1,0:T(8,128)} %bitcast.154, f32[1536]{0:T(1024)S(1)} %copy-done.6, f32[32,64]{1,0:T(8,128)S(1)} %get-tuple-element.64, f32[32,64]{1,0:T(8,128)S(1)} %get-tuple-element.65), kind=kOutput, calls=%fused_computation.53 | convolution fusion | flops 315363328 | bytes 4347904 | tf_op jit(solution)/shard_map/dot_general | solution.py:141
  260.3 17.1 %all_to_all.51 = bf16[32,4,1536]{2,1,0:T(4,128)(2,1)S(1)} all-to-all(bf16[32,4,1536]{2,1,0:T(4,128)(2,1)S(1)} %copy.88), channel_id=1, replica_groups=mesh['groups'=1,'seq'=32] {'seq'}, dimensions={0} | all-to-all | bytes 786432 | tf_op jit(solution)/shard_map/all_to_all | solution.py:147
  277.5 5.1 %fusion.143 = f32[128,3072]{1,0:T(8,128)S(1)} fusion(bf16[128,1536]{1,0:T(8,128)(2,1)S(1)} %squeeze.31, bf16[1536,3072]{1,0:T(8,128)(2,1)} %all-gather.2.cloned.1.call-done), kind=kOutput, calls=%fused_computation.245 | convolution fusion | flops 1207959552 | bytes 11403264 | tf_op jit(solution)/shard_map/dot_general | solution.py:148
  (63 shorter events, 25.1 us)
Async XLA Ops:
  8.7 12.5 %copy-start.4 = (f32[2,64]{1,0:T(2,128)S(1)}, f32[2,64]{1,0:T(2,128)}, u32[]{:S(2)}) copy-start(f32[2,64]{1,0:T(2,128)} %param.8) | copy-start | bytes 1540
  12.7 20.6 %all-to-all-start = ((bf16[32,2,3072]{2,1,0:T(2,128)(2,1)}), bf16[32,2,3072]{2,1,0:T(2,128)(2,1)S(1)}, u32[]{:S(2)}, u32[]{:S(2)}) async-start(bf16[32,2,3072]{2,1,0:T(2,128)(2,1)} %reshape.574), calls=%async_computation | async-start | bytes 786432 | tf_op jit(solution)/shard_map/all_to_all | solution.py:118
  20.0 257.5 %all-gather.2.cloned.1.call-start = ((), (), s32[]{:S(2)}) async-start(), calls=%async_computation.4 | async-start | bytes 9732096 | tf_op jit(solution)/shard_map/all_gather | solution.py:150
  33.6 4.0 %copy-start = (bf16[128,1,1536]{2,1,0:T(2,128)(2,1)}, bf16[128,1,1536]{2,1,0:T(2,128)(2,1)S(1)}, u32[]{:S(2)}) copy-start(bf16[128,1,1536]{2,1,0:T(2,128)(2,1)S(1)} %reshape.575) | copy-start | bytes 1179652
  45.7 3.1 %copy-start.5 = (f32[2,64]{1,0:T(2,128)S(1)}, f32[2,64]{1,0:T(2,128)}, u32[]{:S(2)}) copy-start(f32[2,64]{1,0:T(2,128)} %param.9) | copy-start | bytes 1540
  45.8 112.0 %all-to-all-start.1 = ((f32[2,64,4,1536]{3,2,0,1:T(4,128)}), f32[2,64,4,1536]{3,2,0,1:T(4,128)S(1)}, u32[]{:S(2)}, u32[]{:S(2)}) async-start(f32[2,64,4,1536]{3,2,0,1:T(4,128)} %pad_maximum_fusion), calls=%async_computation.1 | async-start | bytes 6291456 | tf_op jit(solution)/shard_map/all_to_all | solution.py:127
  160.4 5.1 %copy-start.1 = (f32[1,2,128,1536]{2,3,0,1:T(8,128)S(1)}, f32[1,2,128,1536]{2,3,0,1:T(8,128)}, u32[]{:S(2)}) copy-start(f32[1,2,128,1536]{2,3,0,1:T(8,128)} %copy.80) | copy-start | bytes 4718596
  160.4 5.1 %copy-start.2 = (f32[1,2,128,1536]{2,3,0,1:T(8,128)S(1)}, f32[1,2,128,1536]{2,3,0,1:T(8,128)}, u32[]{:S(2)}) copy-start(f32[1,2,128,1536]{2,3,0,1:T(8,128)} %copy.79) | copy-start | bytes 4718596
  165.5 0.9 copy-start.3
  173.3 75.2 %all-to-all-start.2 = ((f32[2,2,128,1536]{3,0,1,2:T(2,128)}), f32[2,2,128,1536]{3,0,1,2:T(2,128)S(1)}, u32[]{:S(2)}, u32[]{:S(2)}) async-start(f32[2,2,128,1536]{3,0,1,2:T(2,128)} %copy.83), calls=%async_computation.2 | async-start | bytes 6291456 | tf_op jit(solution)/shard_map/all_to_all | solution.py:140
  250.7 2.4 copy-start.6
Sparse Core Ops, SparseCore 0:
  23.7 128.8 all-gather.1
where the time goes:
time: 295 us; the launch traced here: 291 us
  waiting for transfers between devices  163 us (55%)
  local copies, waits for them, and re-layouts  31.1 us (11%)
  matrix products  29.7 us (10%)
  other arithmetic  20.6 us (7%)
  blocking collectives  17.1 us (6%)
  starting transfers between devices  14.7 us (5%)
  between operations  14.2 us (5%)
    all_to_all x1, waiting for transfers between devices, shards(): lax.all_to_all(spread, 'seq', split_axis=1, concat_axis=2, tiled=True)  86.4 us
    all_to_all x1, waiting for transfers between devices, shards(): lax.all_to_all(inverse, 'seq', split_axis=2, concat_axis=1, tiled=True)  64.7 us
    all_to_all x1, blocking collectives, shards(): lax.all_to_all(activation, 'seq', split_axis=0, concat_axis=1, tiled=True)  17.1 us
    all_to_all x1, waiting for transfers between devices, shards(): lax.all_to_all(tokens[None], 'seq', split_axis=1, concat_axis=0, tiled=True)  12.1 us
    dot_general x4, matrix products, response(): summed = jnp.dot(cauchy_left, matrix, precision=PRECISE)  8.33 us
    dot_general x2, matrix products, transform(): jnp.einsum('ascb,ckbh->aksh', dft_table_of(length, direction), signal, pr...  7.88 us
    all_to_all x1, starting transfers between devices, shards(): lax.all_to_all(tokens[None], 'seq', split_axis=1, concat_axis=0, tiled=True)  7.33 us
    dot_general x1, matrix products, shards(): jnp.dot(inverse_table, returned.reshape(4 * seq_count, per_device * chann...  6.92 us
  transfers between devices with their start and end apart: 4, of which 3 were waited for; matrix products, arithmetic and copies ran while one was open for 24% of the time, Pallas kernels for 0%

commit v1 on v0

--- a/solution.py
+++ b/solution.py
@@ -1,10 +1,24 @@
+import functools
 import math
 import jax
 import jax.numpy as jnp
 from jax import lax
 from jax.sharding import PartitionSpec as P
+from jax.lax import all_to_all, axis_size
 
 PRECISE = lax.Precision.HIGHEST
+
+
+def flows_replace(s0, where_dim, dim_no):
+    current_value = axis_size("seq")
+    v1 = jnp.split(s0, current_value, axis=where_dim)
+    k_now = jnp.stack(v1, axis=0)
+    view_out = all_to_all(k_now, "seq", split_axis=0, concat_axis=0)
+    t_next = jnp.concatenate(view_out, axis=dim_no)
+    return t_next
+
+
+proceed_wall = functools.partial(flows_replace, where_dim=2, dim_no=1)
 
 
 def phase_of(numerator, period):
@@ -137,7 +151,7 @@
     product = jnp.stack(complex_mul(kernel_pair, (spectrum[0], spectrum[1])))
     inverse = transform(product, tok_rows, -1)
     inverse = twiddled(inverse, pair_here, all_times, full_len, -1)
-    returned = lax.all_to_all(inverse, "seq", split_axis=2, concat_axis=1, tiled=True)
+    returned = proceed_wall(inverse)
     conv_out = jnp.dot(
         inverse_table, returned.reshape(4 * seq_count, per_device * channels), precision=PRECISE
     )

time: 295 us -> 311 us (1.054)
  other arithmetic: 20.6 us -> 41.5 us
  local copies, waits for them, and re-layouts: 31.1 us -> 26.7 us
    unnamed x1 -> x32, other arithmetic: 3.01 us -> 23.2 us
    another operation x1 -> x0, local copies, waits for them, and re-layouts: 3.57 us -> none  [twiddled(): return jnp.stack(turned)]
  transfers between devices with their start and end apart: 4 -> 4, of which waited for: 3 -> 3; matrix products, arithmetic and copies ran while one was open for 24% -> 28% of each run, Pallas kernels for 0% -> 0%
where the time goes in v1:
time: 311 us; the launch traced here: 307 us
  waiting for transfers between devices  163 us (52%)
  other arithmetic  41.5 us (13%)
  matrix products  29.9 us (10%)
  local copies, waits for them, and re-layouts  26.7 us (9%)
  blocking collectives  17.1 us (5%)
  starting transfers between devices  14.6 us (5%)
  between operations  14.2 us (5%)
    all_to_all x1, waiting for transfers between devices, shards(): lax.all_to_all(spread, 'seq', split_axis=1, concat_axis=2, tiled=True)  86.4 us
    all_to_all x1, waiting for transfers between devices, flows_replace(): view_out = all_to_all(k_now, 'seq', split_axis=0, concat_axis=0)  64.7 us
    unnamed x32, other arithmetic  23.2 us
    all_to_all x1, blocking collectives, shards(): lax.all_to_all(activation, 'seq', split_axis=0, concat_axis=1, tiled=True)  17.1 us
    all_to_all x1, waiting for transfers between devices, shards(): lax.all_to_all(tokens[None], 'seq', split_axis=1, concat_axis=0, tiled=True)  12.1 us
    dot_general x4, matrix products, response(): summed = jnp.dot(cauchy_left, matrix, precision=PRECISE)  8.32 us
    dot_general x2, matrix products, transform(): jnp.einsum('ascb,ckbh->aksh', dft_table_of(length, direction), signal, pr...  8.05 us
    all_to_all x1, starting transfers between devices, shards(): lax.all_to_all(tokens[None], 'seq', split_axis=1, concat_axis=0, tiled=True)  7.33 us
  transfers between devices with their start and end apart: 4, of which 3 were waited for; matrix products, arithmetic and copies ran while one was open for 28% of the time, Pallas kernels for 0%

profile of v1, /device:TPU:0, one launch (start us, length us, event | category | flops | bytes accessed | tf_op | source)
XLA Modules:
  0.0 307.3 jit_solution(6931523813743567248)
XLA Ops:
  8.7 3.0 reduce.4
  12.7 7.3 %all-to-all-start = ((bf16[32,2,3072]{2,1,0:T(2,128)(2,1)}), bf16[32,2,3072]{2,1,0:T(2,128)(2,1)S(1)}, u32[]{:S(2)}, u32[]{:S(2)}) async-start(bf16[32,2,3072]{2,1,0:T(2,128)(2,1)} %reshape.573), calls=%async_computation | async-start | bytes 786432 | tf_op jit(solution)/shard_map/all_to_all | solution.py:132
  21.2 12.1 %all-to-all-done = bf16[32,2,3072]{2,1,0:T(2,128)(2,1)S(1)} async-done(((bf16[32,2,3072]{2,1,0:T(2,128)(2,1)}), bf16[32,2,3072]{2,1,0:T(2,128)(2,1)S(1)}, u32[]{:S(2)}, u32[]{:S(2)}) %all-to-all-start) | async-done | bytes 393248 | tf_op jit(solution)/shard_map/all_to_all | solution.py:132
  33.6 2.2 bitcast_reduce_fusion
  40.1 2.4 squeeze.30
  43.3 2.5 pad_maximum_fusion
  45.7 3.1 %all-to-all-start.1 = ((f32[2,64,4,1536]{3,2,0,1:T(4,128)}), f32[2,64,4,1536]{3,2,0,1:T(4,128)S(1)}, u32[]{:S(2)}, u32[]{:S(2)}) async-start(f32[2,64,4,1536]{3,2,0,1:T(4,128)} %pad_maximum_fusion), calls=%async_computation.1 | async-start | bytes 6291456 | tf_op jit(solution)/shard_map/all_to_all | solution.py:141
  51.1 2.7 fusion.12
  53.8 2.7 fusion.20
  56.5 2.7 fusion.4
  63.5 3.0 copy.79
  66.5 3.0 copy.78
  71.3 86.4 %all-to-all-done.1 = f32[2,64,4,1536]{3,2,0,1:T(4,128)S(1)} async-done(((f32[2,64,4,1536]{3,2,0,1:T(4,128)}), f32[2,64,4,1536]{3,2,0,1:T(4,128)S(1)}, u32[]{:S(2)}, u32[]{:S(2)}) %all-to-all-start.1) | async-done | bytes 3145760 | tf_op jit(solution)/shard_map/all_to_all | solution.py:141
  157.7 2.6 copy.76
  160.4 5.1 %convolution_bitcast_fusion.1 = f32[2,2,128,1536]{2,3,0,1:T(8,128)S(1)} fusion(f32[2,2,128,1536,1]{3,1,2,0,4:T(2,128)S(1)} %bitcast.213, f32[1,128,2,128]{3,1,2,0:T(8,128)S(1)} %get-tuple-element.41, f32[1,128,2,128]{3,1,2,0:T(8,128)S(1)} %get-tuple-element.40), kind=kOutput, calls=%fused_computation.63 | convolution fusion | flops 2415984640 | bytes 6553600 | tf_op jit(solution)/shard_map/ascb,ckbh->aksh/dot_general | solution.py:102
  166.4 3.0 convolution_bitcast_fusion
  190.8 3.6 %all-to-all-start.2 = ((f32[32,2,2,4,1536]{4,3,1,2,0:T(4,128)}), f32[32,2,2,4,1536]{4,3,1,2,0:T(4,128)S(1)}, u32[]{:S(2)}, u32[]{:S(2)}) async-start(f32[32,2,2,4,1536]{4,3,1,2,0:T(4,128)} %fusion.87), calls=%async_computation.2 | async-start | bytes 6291456 | tf_op jit(solution)/shard_map/all_to_all | solution.py:16
  194.4 4.3 %convert_reduce_fusion = f32[128,1536]{1,0:T(8,128)} fusion(bf16[128,1,1536]{2,1,0:T(2,128)(2,1)} %copy-done), kind=kLoop, calls=%fused_computation.121 | loop fusion | flops 196608 | bytes 1179648 | tf_op jit(solution)/shard_map/convert_element_type | solution.py:135
  198.7 2.3 reshape.563
  201.0 64.7 %all-to-all-done.2 = f32[32,2,2,4,1536]{4,3,1,2,0:T(4,128)S(1)} async-done(((f32[32,2,2,4,1536]{4,3,1,2,0:T(4,128)}), f32[32,2,2,4,1536]{4,3,1,2,0:T(4,128)S(1)}, u32[]{:S(2)}, u32[]{:S(2)}) %all-to-all-start.2) | async-done | bytes 3145760 | tf_op jit(solution)/shard_map/all_to_all | solution.py:16
  267.2 2.4 copy.84
  269.5 6.9 %fusion.32 = bf16[32,4,1536]{2,0,1:T(8,128)(2,1)S(1)} fusion(f32[32,4,1536]{2,1,0:T(4,128)} %reshape.563, f32[4,1536,128]{2,1,0:T(8,128)} %bitcast.218, f32[1536]{0:T(1024)S(1)} %copy-done.6, f32[32,64]{1,0:T(8,128)S(1)} %get-tuple-element.64, f32[32,64]{1,0:T(8,128)S(1)} %get-tuple-element.65), kind=kOutput, calls=%fused_computation.114 | convolution fusion | flops 315363328 | bytes 4347904 | tf_op jit(solution)/shard_map/dot_general | solution.py:155
  276.8 17.1 %all_to_all.41 = bf16[32,4,1536]{2,1,0:T(4,128)(2,1)S(1)} all-to-all(bf16[32,4,1536]{2,1,0:T(4,128)(2,1)S(1)} %copy.86), channel_id=1, replica_groups=mesh['groups'=1,'seq'=32] {'seq'}, dimensions={0} | all-to-all | bytes 786432 | tf_op jit(solution)/shard_map/all_to_all | solution.py:161
  294.0 5.1 %fusion.176 = f32[128,3072]{1,0:T(8,128)S(1)} fusion(bf16[128,1536]{1,0:T(8,128)(2,1)S(1)} %squeeze.31, bf16[1536,3072]{1,0:T(8,128)(2,1)} %all-gather.2.cloned.1.call-done), kind=kOutput, calls=%fused_computation.371 | convolution fusion | flops 1207959552 | bytes 11403264 | tf_op jit(solution)/shard_map/dot_general | solution.py:162
  (93 shorter events, 43.0 us)
Async XLA Ops:
  6.5 14.6 %copy-start.4 = (f32[2,64]{1,0:T(2,128)S(1)}, f32[2,64]{1,0:T(2,128)}, u32[]{:S(2)}) copy-start(f32[2,64]{1,0:T(2,128)} %param.8) | copy-start | bytes 1540
  12.7 20.6 %all-to-all-start = ((bf16[32,2,3072]{2,1,0:T(2,128)(2,1)}), bf16[32,2,3072]{2,1,0:T(2,128)(2,1)S(1)}, u32[]{:S(2)}, u32[]{:S(2)}) async-start(bf16[32,2,3072]{2,1,0:T(2,128)(2,1)} %reshape.573), calls=%async_computation | async-start | bytes 786432 | tf_op jit(solution)/shard_map/all_to_all | solution.py:132
  20.0 274.0 %all-gather.2.cloned.1.call-start = ((), (), s32[]{:S(2)}) async-start(), calls=%async_computation.4 | async-start | bytes 9732096 | tf_op jit(solution)/shard_map/all_gather | solution.py:164
  33.6 5.4 %copy-start = (bf16[128,1,1536]{2,1,0:T(2,128)(2,1)}, bf16[128,1,1536]{2,1,0:T(2,128)(2,1)S(1)}, u32[]{:S(2)}) copy-start(bf16[128,1,1536]{2,1,0:T(2,128)(2,1)S(1)} %reshape.574) | copy-start | bytes 1179652
  45.7 3.1 %copy-start.5 = (f32[2,64]{1,0:T(2,128)S(1)}, f32[2,64]{1,0:T(2,128)}, u32[]{:S(2)}) copy-start(f32[2,64]{1,0:T(2,128)} %param.9) | copy-start | bytes 1540
  45.7 112.0 %all-to-all-start.1 = ((f32[2,64,4,1536]{3,2,0,1:T(4,128)}), f32[2,64,4,1536]{3,2,0,1:T(4,128)S(1)}, u32[]{:S(2)}, u32[]{:S(2)}) async-start(f32[2,64,4,1536]{3,2,0,1:T(4,128)} %pad_maximum_fusion), calls=%async_computation.1 | async-start | bytes 6291456 | tf_op jit(solution)/shard_map/all_to_all | solution.py:141
  160.4 5.1 %copy-start.1 = (f32[1,2,128,1536]{2,3,0,1:T(8,128)S(1)}, f32[1,2,128,1536]{2,3,0,1:T(8,128)}, u32[]{:S(2)}) copy-start(f32[1,2,128,1536]{2,3,0,1:T(8,128)} %copy.79) | copy-start | bytes 4718596
  160.4 5.1 %copy-start.2 = (f32[1,2,128,1536]{2,3,0,1:T(8,128)S(1)}, f32[1,2,128,1536]{2,3,0,1:T(8,128)}, u32[]{:S(2)}) copy-start(f32[1,2,128,1536]{2,3,0,1:T(8,128)} %copy.78) | copy-start | bytes 4718596
  165.5 0.9 copy-start.3
  190.8 74.9 %all-to-all-start.2 = ((f32[32,2,2,4,1536]{4,3,1,2,0:T(4,128)}), f32[32,2,2,4,1536]{4,3,1,2,0:T(4,128)S(1)}, u32[]{:S(2)}, u32[]{:S(2)}) async-start(f32[32,2,2,4,1536]{4,3,1,2,0:T(4,128)} %fusion.87), calls=%async_computation.2 | async-start | bytes 6291456 | tf_op jit(solution)/shard_map/all_to_all | solution.py:16
  267.2 2.4 copy-start.6
Sparse Core Ops, SparseCore 0:
  23.7 128.8 all-gather.1
